TPU v7x, 128 devices: a whole 4x4x4 slice. The times are simulated.
128 devices in a mesh: ctx: 64 (over z, x, y), wsh: 2 (over core).
Axes of the slice: x: 4, y: 4, z: 4, core: 2. Of those that a mesh axis runs over, the one named last changes fastest.
Arguments:
- block_input: bfloat16 [2, 8192, 640], P('wsh', 'ctx'), may hold values from -6 to 6
- cotangent: float32 [2, 8192, 640], P('wsh', 'ctx'), may hold values from -6 to 6
- pair_blocks: int32 [64, 2], replicated, may hold values from 0 to 127, as said below
- w_query: bfloat16 [640, 1024], P(None, 'wsh'), may hold values from -0.25 to 0.25
- w_key: bfloat16 [640, 256], P(None, 'wsh'), may hold values from -0.25 to 0.25
- w_value: bfloat16 [640, 256], P(None, 'wsh'), may hold values from -0.25 to 0.25
- w_out: bfloat16 [1024, 640], P('wsh'), may hold values from -0.1875 to 0.1875
- w_gate: bfloat16 [640, 2048], P(None, 'wsh'), may hold values from -0.25 to 0.25
- w_up: bfloat16 [640, 2048], P(None, 'wsh'), may hold values from -0.25 to 0.25
- w_down: bfloat16 [2048, 640], P('wsh'), may hold values from -0.125 to 0.125
- attn_pre_gain: bfloat16 [640], P('wsh'), may hold values from -0.3984375 to 0.59765625
- query_gain: bfloat16 [256], P('wsh'), may hold values from -0.3984375 to 0.59765625
- key_gain: bfloat16 [256], P('wsh'), may hold values from -0.3984375 to 0.59765625
- attn_post_gain: bfloat16 [640], P('wsh'), may hold values from -0.3984375 to 0.59765625
- ffw_pre_gain: bfloat16 [640], P('wsh'), may hold values from -0.3984375 to 0.59765625
- ffw_post_gain: bfloat16 [640], P('wsh'), may hold values from -0.3984375 to 0.59765625
Outputs:
- block_output: float32 [2, 8192, 640], P('wsh', 'ctx')
- input_grad: float32 [2, 8192, 640], P('wsh', 'ctx')
- w_query_grad: float32 [640, 1024], P(None, 'wsh')
- w_key_grad: float32 [640, 256], P(None, 'wsh')
- w_value_grad: float32 [640, 256], P(None, 'wsh')
- w_out_grad: float32 [1024, 640], P('wsh')
- w_gate_grad: float32 [640, 2048], P(None, 'wsh')
- w_up_grad: float32 [640, 2048], P(None, 'wsh')
- w_down_grad: float32 [2048, 640], P('wsh')
- attn_pre_gain_grad: float32 [640], P('wsh')
- query_gain_grad: float32 [256], P('wsh')
- key_gain_grad: float32 [256], P('wsh')
- attn_post_gain_grad: float32 [640], P('wsh')
- ffw_pre_gain_grad: float32 [640], P('wsh')
- ffw_post_gain_grad: float32 [640], P('wsh')
Inputs may be any that keep to these rules, and one draw needn't show every extreme that they name: `pair_blocks`: row r holds a block b and its mirror 2 * 64 - 1 - b, in the order in which index r of ctx stores them; over all rows every one of the 128 blocks appears exactly once.
All inputs are finite; a program needn't handle non-finite values.
Results may differ from a plain program's by a relative error of at most 0.018.
Values may be sent and summed in bfloat16 or wider, within the bound.
No kernel may reach another device: no remote copies, remote signals or barrier semaphores. Data moves between devices by JAX's collectives and lax.ppermute only.
A program may use at most 192 MiB of HBM per device.

v0:
```python
import jax
import jax.numpy as jnp
from jax import lax
from jax.sharding import PartitionSpec as P

HEADS = 4
HDIM = 256


epsilon = 1e-06
theta_base = 1000000.0


def rms_forward(values, gain_w):
    factor = lax.rsqrt(jnp.mean(values * values, axis=-1, keepdims=True) + epsilon)
    return (values * factor * (1.0 + gain_w), factor)


def rms_backward(values, factor, gain_w, grad_out):
    weighted = grad_out * (1.0 + gain_w)
    inner = jnp.mean(weighted * values, axis=-1, keepdims=True)
    grad_in = factor * (weighted - values * factor * factor * inner)
    grad_gain = jnp.sum((grad_out * values * factor).reshape(-1, values.shape[-1]), axis=0)
    return (grad_in, grad_gain)


def rotary_tables(positions, width):
    half_width = width // 2
    frequency = theta_base ** (-jnp.arange(half_width, dtype=jnp.float32) * 2.0 / width)
    angles = positions.astype(jnp.float32)[:, None] * frequency[None, :]
    return (jnp.cos(angles)[:, None, :], jnp.sin(angles)[:, None, :])


def rotate(values, cos_tab, sin_tab):
    half_width = values.shape[-1] // 2
    first_half = values[..., :half_width]
    second_half = values[..., half_width:]
    return jnp.concatenate(
        [
            first_half * cos_tab - second_half * sin_tab,
            second_half * cos_tab + first_half * sin_tab,
        ],
        axis=-1,
    )


def rotate_back(grads, cos_tab, sin_tab):
    half_width = grads.shape[-1] // 2
    first_half = grads[..., :half_width]
    second_half = grads[..., half_width:]
    return jnp.concatenate(
        [
            first_half * cos_tab + second_half * sin_tab,
            second_half * cos_tab - first_half * sin_tab,
        ],
        axis=-1,
    )


def block_positions(block_ids, half_rows):
    offsets = jnp.arange(half_rows, dtype=jnp.int32)
    return (block_ids[:, None] * half_rows + offsets[None, :]).reshape(-1)


def dot_f32(left, right):
    return jnp.dot(left, right, preferred_element_type=jnp.float32)


def masked_scores(query_rot, key_all, query_pos, key_pos):
    scores = jnp.einsum(
        "qhd,kd->hqk", query_rot, key_all, preferred_element_type=jnp.float32
    ) * HDIM ** (-0.5)
    return jnp.where(key_pos[None, None, :] <= query_pos[None, :, None], scores, -1e30)


def per_device(
    block_input,
    cotangent,
    pair_blocks,
    w_query,
    w_key,
    w_value,
    w_out,
    w_gate,
    w_up,
    w_down,
    attn_pre_gain,
    query_gain,
    key_gain,
    attn_post_gain,
    ffw_pre_gain,
    ffw_post_gain,
):
    row_count = block_input.shape[1]
    half_rows = row_count // 2
    my_rank = lax.axis_index("ctx")
    resid_in = block_input[0].astype(jnp.float32)
    grad_top = cotangent[0]
    my_blocks = lax.dynamic_slice_in_dim(pair_blocks, my_rank, 1, 0)[0]
    query_pos = block_positions(my_blocks, half_rows)
    key_pos = block_positions(pair_blocks.reshape(-1), half_rows)
    cos_tab, sin_tab = rotary_tables(query_pos, HDIM)
    (
        query_w,
        key_w,
        value_w,
        out_w,
        gate_w,
        up_w,
        down_w,
        gain_one,
        gain_query,
        gain_key,
        gain_two,
        gain_three,
        gain_four,
    ) = (
        lax.all_gather(w_query, "wsh", axis=1, tiled=True),
        lax.all_gather(w_key, "wsh", axis=1, tiled=True),
        lax.all_gather(w_value, "wsh", axis=1, tiled=True),
        lax.all_gather(w_out, "wsh", axis=0, tiled=True),
        lax.all_gather(w_gate, "wsh", axis=1, tiled=True),
        lax.all_gather(w_up, "wsh", axis=1, tiled=True),
        lax.all_gather(w_down, "wsh", axis=0, tiled=True),
        lax.all_gather(attn_pre_gain, "wsh", axis=0, tiled=True),
        lax.all_gather(query_gain, "wsh", axis=0, tiled=True),
        lax.all_gather(key_gain, "wsh", axis=0, tiled=True),
        lax.all_gather(attn_post_gain, "wsh", axis=0, tiled=True),
        lax.all_gather(ffw_pre_gain, "wsh", axis=0, tiled=True),
        lax.all_gather(ffw_post_gain, "wsh", axis=0, tiled=True),
    )
    gain_one = gain_one.astype(jnp.float32)
    gain_query = gain_query.astype(jnp.float32)
    gain_key = gain_key.astype(jnp.float32)
    gain_two = gain_two.astype(jnp.float32)
    normed_one, factor_one = rms_forward(resid_in, gain_one)
    attn_in = normed_one.astype(jnp.bfloat16)
    query_raw = dot_f32(attn_in, query_w).reshape(row_count, HEADS, HDIM)
    key_raw = dot_f32(attn_in, key_w)[:, None, :]
    value_bf = dot_f32(attn_in, value_w).astype(jnp.bfloat16)
    query_normed, query_factor = rms_forward(query_raw, gain_query)
    key_normed, key_factor = rms_forward(key_raw, gain_key)
    query_rot = rotate(query_normed, cos_tab, sin_tab).astype(jnp.bfloat16)
    key_rot = rotate(key_normed, cos_tab, sin_tab)[:, 0, :].astype(jnp.bfloat16)
    key_all, value_all = (
        lax.all_gather(key_rot, "ctx", axis=0, tiled=True),
        lax.all_gather(value_bf, "ctx", axis=0, tiled=True),
    )
    scores = masked_scores(query_rot, key_all, query_pos, key_pos)
    top_score = jnp.max(scores, axis=-1, keepdims=True)
    shifted = jnp.exp(scores - top_score)
    totals = jnp.sum(shifted, axis=-1, keepdims=True)
    probs = (shifted / totals).astype(jnp.bfloat16)
    log_total = top_score[..., 0] + jnp.log(totals[..., 0])
    attn_heads = jnp.einsum(
        "hqk,kd->qhd", probs, value_all, preferred_element_type=jnp.float32
    ).astype(jnp.bfloat16)
    attn_out = attn_heads.reshape(row_count, HEADS * HDIM)
    attn_proj = dot_f32(attn_out, out_w)
    normed_two, factor_two = rms_forward(attn_proj, gain_two)
    mid = resid_in + normed_two
    gain_three = gain_three.astype(jnp.float32)
    gain_four = gain_four.astype(jnp.float32)
    normed_three, factor_three = rms_forward(mid, gain_three)
    ffw_in = normed_three.astype(jnp.bfloat16)
    gate = dot_f32(ffw_in, gate_w)
    up_val = dot_f32(ffw_in, up_w)
    activated, gelu_back = jax.vjp(lambda inner: jax.nn.gelu(inner, approximate=True), gate)
    hidden = (activated * up_val).astype(jnp.bfloat16)
    ffw_proj = dot_f32(hidden, down_w)
    normed_four, factor_four = rms_forward(ffw_proj, gain_four)
    block_output = mid + normed_four
    grad_ffw, grad_gain_four = rms_backward(ffw_proj, factor_four, gain_four, grad_top)
    grad_ffw_bf = grad_ffw.astype(jnp.bfloat16)
    grad_w_down = dot_f32(hidden.T, grad_ffw_bf)
    grad_hidden = dot_f32(grad_ffw_bf, down_w.T)
    grad_gate = gelu_back(grad_hidden * up_val)[0].astype(jnp.bfloat16)
    grad_up = (grad_hidden * activated).astype(jnp.bfloat16)
    grad_w_gate = dot_f32(ffw_in.T, grad_gate)
    grad_w_up = dot_f32(ffw_in.T, grad_up)
    grad_ffw_in = dot_f32(grad_gate, gate_w.T) + dot_f32(grad_up, up_w.T)
    grad_mid_part, grad_gain_three = rms_backward(mid, factor_three, gain_three, grad_ffw_in)
    grad_mid = grad_top + grad_mid_part
    grad_proj, grad_gain_two = rms_backward(attn_proj, factor_two, gain_two, grad_mid)
    grad_proj_bf = grad_proj.astype(jnp.bfloat16)
    grad_w_out = dot_f32(attn_out.T, grad_proj_bf)
    grad_attn = dot_f32(grad_proj_bf, out_w.T).astype(jnp.bfloat16)
    grad_heads = grad_attn.reshape(row_count, HEADS, HDIM)
    delta = jnp.sum(grad_heads.astype(jnp.float32) * attn_heads.astype(jnp.float32), axis=-1).T
    scores_again = masked_scores(query_rot, key_all, query_pos, key_pos)
    probs_again = jnp.exp(scores_again - log_total[:, :, None])
    grad_probs = jnp.einsum(
        "qhd,kd->hqk", grad_heads, value_all, preferred_element_type=jnp.float32
    )
    grad_scores = (probs_again * (grad_probs - delta[:, :, None])).astype(jnp.bfloat16)
    grad_query = jnp.einsum(
        "hqk,kd->qhd", grad_scores, key_all, preferred_element_type=jnp.float32
    ) * HDIM ** (-0.5)
    grad_key_part = jnp.einsum(
        "hqk,qhd->kd", grad_scores, query_rot, preferred_element_type=jnp.float32
    ) * HDIM ** (-0.5)
    grad_value_part = jnp.einsum(
        "hqk,qhd->kd",
        probs_again.astype(jnp.bfloat16),
        grad_heads,
        preferred_element_type=jnp.float32,
    )
    kv_terms = jnp.concatenate([grad_key_part, grad_value_part], axis=1)
    kv_mine = lax.psum_scatter(kv_terms, "ctx", scatter_dimension=0, tiled=True)
    grad_key = kv_mine[:, :HDIM]
    grad_value = kv_mine[:, HDIM:]
    grad_query_raw, grad_gain_query = rms_backward(
        query_raw, query_factor, gain_query, rotate_back(grad_query, cos_tab, sin_tab)
    )
    grad_key_raw, grad_gain_key = rms_backward(
        key_raw, key_factor, gain_key, rotate_back(grad_key[:, None, :], cos_tab, sin_tab)
    )
    grad_query_bf = grad_query_raw.reshape(row_count, HEADS * HDIM).astype(jnp.bfloat16)
    grad_key_bf = grad_key_raw[:, 0, :].astype(jnp.bfloat16)
    grad_value_bf = grad_value.astype(jnp.bfloat16)
    grad_w_query = dot_f32(attn_in.T, grad_query_bf)
    grad_w_key = dot_f32(attn_in.T, grad_key_bf)
    grad_w_value = dot_f32(attn_in.T, grad_value_bf)
    grad_attn_in = (
        dot_f32(grad_query_bf, query_w.T)
        + dot_f32(grad_key_bf, key_w.T)
        + dot_f32(grad_value_bf, value_w.T)
    )
    grad_in_part, grad_gain_one = rms_backward(resid_in, factor_one, gain_one, grad_attn_in)
    input_grad = grad_mid + grad_in_part
    (
        half_query,
        half_key,
        half_value,
        half_out,
        half_gate,
        half_up,
        half_down,
        half_one,
        half_qgain,
        half_kgain,
        half_two,
        half_three,
        half_four,
    ) = (
        lax.psum_scatter(
            grad_w_query.astype(jnp.bfloat16), "wsh", scatter_dimension=1, tiled=True
        ).astype(jnp.float32),
        lax.psum_scatter(
            grad_w_key.astype(jnp.bfloat16), "wsh", scatter_dimension=1, tiled=True
        ).astype(jnp.float32),
        lax.psum_scatter(
            grad_w_value.astype(jnp.bfloat16), "wsh", scatter_dimension=1, tiled=True
        ).astype(jnp.float32),
        lax.psum_scatter(
            grad_w_out.astype(jnp.bfloat16), "wsh", scatter_dimension=0, tiled=True
        ).astype(jnp.float32),
        lax.psum_scatter(
            grad_w_gate.astype(jnp.bfloat16), "wsh", scatter_dimension=1, tiled=True
        ).astype(jnp.float32),
        lax.psum_scatter(
            grad_w_up.astype(jnp.bfloat16), "wsh", scatter_dimension=1, tiled=True
        ).astype(jnp.float32),
        lax.psum_scatter(
            grad_w_down.astype(jnp.bfloat16), "wsh", scatter_dimension=0, tiled=True
        ).astype(jnp.float32),
        lax.psum_scatter(
            grad_gain_one.astype(jnp.bfloat16), "wsh", scatter_dimension=0, tiled=True
        ).astype(jnp.float32),
        lax.psum_scatter(
            grad_gain_query.astype(jnp.bfloat16), "wsh", scatter_dimension=0, tiled=True
        ).astype(jnp.float32),
        lax.psum_scatter(
            grad_gain_key.astype(jnp.bfloat16), "wsh", scatter_dimension=0, tiled=True
        ).astype(jnp.float32),
        lax.psum_scatter(
            grad_gain_two.astype(jnp.bfloat16), "wsh", scatter_dimension=0, tiled=True
        ).astype(jnp.float32),
        lax.psum_scatter(
            grad_gain_three.astype(jnp.bfloat16), "wsh", scatter_dimension=0, tiled=True
        ).astype(jnp.float32),
        lax.psum_scatter(
            grad_gain_four.astype(jnp.bfloat16), "wsh", scatter_dimension=0, tiled=True
        ).astype(jnp.float32),
    )
    (
        sum_query,
        sum_key,
        sum_value,
        sum_out,
        sum_gate,
        sum_up,
        sum_down,
        sum_one,
        sum_qgain,
        sum_kgain,
        sum_two,
        sum_three,
        sum_four,
    ) = lax.psum(
        (
            half_query,
            half_key,
            half_value,
            half_out,
            half_gate,
            half_up,
            half_down,
            half_one,
            half_qgain,
            half_kgain,
            half_two,
            half_three,
            half_four,
        ),
        "ctx",
    )
    return (
        block_output[None],
        input_grad[None],
        sum_query,
        sum_key,
        sum_value,
        sum_out,
        sum_gate,
        sum_up,
        sum_down,
        sum_one,
        sum_qgain,
        sum_kgain,
        sum_two,
        sum_three,
        sum_four,
    )


def solution(mesh):
    return jax.shard_map(
        per_device,
        mesh=mesh,
        in_specs=(
            P("wsh", "ctx", None),
            P("wsh", "ctx", None),
            P(),
            P(None, "wsh"),
            P(None, "wsh"),
            P(None, "wsh"),
            P("wsh", None),
            P(None, "wsh"),
            P(None, "wsh"),
            P("wsh", None),
            P("wsh"),
            P("wsh"),
            P("wsh"),
            P("wsh"),
            P("wsh"),
            P("wsh"),
        ),
        out_specs=(
            P("wsh", "ctx", None),
            P("wsh", "ctx", None),
            P(None, "wsh"),
            P(None, "wsh"),
            P(None, "wsh"),
            P("wsh", None),
            P(None, "wsh"),
            P(None, "wsh"),
            P("wsh", None),
            P("wsh"),
            P("wsh"),
            P("wsh"),
            P("wsh"),
            P("wsh"),
            P("wsh"),
        ),
        check_vma=False,
    )
```

profile of v0, /device:TPU:0, one launch (start us, length us, event | category | flops | bytes accessed | tf_op | source)
XLA Modules:
  0.0 1201.1 jit_solution(14206055669539594924)
XLA Ops:
  35.8 4.4 broadcast_compare_fusion
  43.0 55.2 %all-gather.23.cloned.1.call-done = bf16[8192,1,256]{2,0,1:T(8,128)(2,1)} async-done(((bf16[128,1,256]{2,0,1:T(8,128)(2,1)}), bf16[8192,1,256]{2,0,1:T(8,128)(2,1)}) %all-gather.23.cloned.1.call-update) | async-done | bytes 4194320 | tf_op jit(solution)/shard_map/all_gather | solution.py:146
  98.1 10.1 fusion.81
  108.3 8.0 fusion.2
  116.4 51.7 %all-gather.11.cloned.1.call-done = bf16[8192,256]{1,0:T(8,128)(2,1)} async-done(((bf16[128,256]{1,0:T(8,128)(2,1)}), bf16[8192,256]{1,0:T(8,128)(2,1)}) %all-gather.11.cloned.1.call-update) | async-done | bytes 4194320 | tf_op jit(solution)/shard_map/all_gather | solution.py:147
  168.1 9.7 fusion.19
  181.3 14.8 %all-gather.17.cloned.1.call-done = bf16[640,2048]{1,0:T(8,128)(2,1)} async-done(((bf16[640,1024]{1,0:T(8,128)(2,1)}), bf16[640,2048]{1,0:T(8,128)(2,1)}) %all-gather.17.cloned.1.call-update) | async-done | bytes 2621456 | tf_op jit(solution)/shard_map/all_gather | solution.py:122
  198.4 14.7 %all-gather.19.cloned.1.call-done = bf16[640,2048]{1,0:T(8,128)(2,1)} async-done(((bf16[640,1024]{1,0:T(8,128)(2,1)}), bf16[640,2048]{1,0:T(8,128)(2,1)}) %all-gather.19.cloned.1.call-update) | async-done | bytes 2621456 | tf_op jit(solution)/shard_map/all_gather | solution.py:123
  213.0 3.5 multiply_convert_fusion.1
  216.5 13.6 %all-gather.21.cloned.1.call-done = bf16[2048,640]{1,0:T(8,128)(2,1)} async-done(((bf16[1024,640]{1,0:T(8,128)(2,1)}), bf16[2048,640]{1,0:T(8,128)(2,1)}) %all-gather.21.cloned.1.call-update) | async-done | bytes 2621456 | tf_op jit(solution)/shard_map/all_gather | solution.py:124
  241.6 11.6 convolution_bitcast_fusion
  253.2 8.8 fusion.1
  262.0 3.8 fusion.4
  268.6 6.3 pad_maximum_fusion
  274.9 8.0 fusion.16
  296.5 368.9 %reduce-scatter.13.cloned.1.call-done = f32[128,512]{1,0:T(8,128)} async-done(((f32[8192,512]{1,0:T(8,128)}), f32[128,512]{1,0:T(8,128)}) %reduce-scatter.13.cloned.1.call-update) | async-done | bytes 262160 | tf_op jit(solution)/shard_map/reduce_scatter | solution.py:209
  669.0 5.5 reduce-scatter.15.cloned.1.call-done
  674.5 15.8 %reduce-scatter.17.cloned.1.call-done = bf16[512,640]{1,0:T(8,128)(2,1)} async-done(((bf16[1024,640]{1,0:T(8,128)(2,1)}), bf16[512,640]{1,0:T(8,128)(2,1)}) %reduce-scatter.17.cloned.1.call-update) | async-done | bytes 655376 | tf_op jit(solution)/shard_map/reduce_scatter | solution.py:255
  690.3 17.2 %reduce-scatter.19.cloned.1.call-done = bf16[640,1024]{1,0:T(8,128)(2,1)} async-done(((bf16[640,2048]{1,0:T(8,128)(2,1)}), bf16[640,1024]{1,0:T(8,128)(2,1)}) %reduce-scatter.19.cloned.1.call-update) | async-done | bytes 1310736 | tf_op jit(solution)/shard_map/reduce_scatter | solution.py:258
  707.5 17.2 %reduce-scatter.21.cloned.1.call-done = bf16[640,1024]{1,0:T(8,128)(2,1)} async-done(((bf16[640,2048]{1,0:T(8,128)(2,1)}), bf16[640,1024]{1,0:T(8,128)(2,1)}) %reduce-scatter.21.cloned.1.call-update) | async-done | bytes 1310736 | tf_op jit(solution)/shard_map/reduce_scatter | solution.py:261
  724.7 17.2 %reduce-scatter.23.cloned.1.call-done = bf16[1024,640]{1,0:T(8,128)(2,1)} async-done(((bf16[2048,640]{1,0:T(8,128)(2,1)}), bf16[1024,640]{1,0:T(8,128)(2,1)}) %reduce-scatter.23.cloned.1.call-update) | async-done | bytes 1310736 | tf_op jit(solution)/shard_map/reduce_scatter | solution.py:264
  750.3 5.8 reduce-scatter.25.cloned.1.call-done
  757.1 13.5 %reduce-scatter.27.cloned.1.call-done = bf16[128,640]{1,0:T(8,128)(2,1)} async-done(((bf16[256,640]{1,0:T(8,128)(2,1)}), bf16[128,640]{1,0:T(8,128)(2,1)}) %reduce-scatter.27.cloned.1.call-update) | async-done | bytes 163856
  771.7 422.5 %all-reduce.14 = (f32[640,512]{1,0:T(8,128)}, f32[640,128]{1,0:T(8,128)}, f32[640,128]{1,0:T(8,128)}, f32[512,640]{1,0:T(8,128)}, f32[640,1024]{1,0:T(8,128)}, /...) all-reduce(bf16[640,512]{1,0:T(8,128)(2,1)} %reduce-scatter.15.clon, ...), channel_id=1, replica_groups=mesh['ctx'=64,'wsh'=2] {'ctx'}, use_global_device_ids=true, to_apply=%region_17.18 | all-reduce | flops 2786816 | bytes 16723968 | tf_op jit(solution)/shard_map/psum | solution.py:300
  (226 shorter events, 76.2 us)
Async XLA Ops:
  7.2 33.1 %all-gather.13.cloned.1.call-start = ((), (), s32[]{:S(2)}) async-start(), calls=%async_computation.9 | async-start | bytes 1966080 | tf_op jit(solution)/shard_map/all_gather | solution.py:118
  7.9 90.2 %all-gather.23.cloned.1.call-start = ((), (), s32[]{:S(2)}) async-start(), calls=%async_computation.20 | async-start | bytes 4259840 | tf_op jit(solution)/shard_map/all_gather | solution.py:146
  25.9 142.2 %all-gather.11.cloned.1.call-start = ((), (), s32[]{:S(2)}) async-start(), calls=%async_computation.8 | async-start | bytes 4259840 | tf_op jit(solution)/shard_map/all_gather | solution.py:147
  30.7 148.4 %all-gather.15.cloned.1.call-start = ((), (), s32[]{:S(2)}) async-start(), calls=%async_computation.10 | async-start | bytes 1966080 | tf_op jit(solution)/shard_map/all_gather | solution.py:121
  31.3 164.7 %all-gather.17.cloned.1.call-start = ((), (), s32[]{:S(2)}) async-start(), calls=%async_computation.11 | async-start | bytes 3932160 | tf_op jit(solution)/shard_map/all_gather | solution.py:122
  31.9 181.1 %all-gather.19.cloned.1.call-start = ((), (), s32[]{:S(2)}) async-start(), calls=%async_computation.12 | async-start | bytes 3932160 | tf_op jit(solution)/shard_map/all_gather | solution.py:123
  32.5 197.6 %all-gather.21.cloned.1.call-start = ((), (), s32[]{:S(2)}) async-start(), calls=%async_computation.13 | async-start | bytes 3932160 | tf_op jit(solution)/shard_map/all_gather | solution.py:124
  33.2 632.2 %reduce-scatter.13.cloned.1.call-start = ((), (), s32[]{:S(2)}) async-start(), calls=%async_computation.14 | async-start | bytes 17039360 | tf_op jit(solution)/shard_map/reduce_scatter | solution.py:209
  274.9 399.6 %reduce-scatter.15.cloned.1.call-start = ((), (), s32[]{:S(2)}) async-start(), calls=%async_computation.15 | async-start | bytes 1966080 | tf_op jit(solution)/shard_map/reduce_scatter | solution.py:246
  285.9 404.4 %reduce-scatter.17.cloned.1.call-start = ((), (), s32[]{:S(2)}) async-start(), calls=%async_computation.16 | async-start | bytes 1966080 | tf_op jit(solution)/shard_map/reduce_scatter | solution.py:255
  287.5 420.0 %reduce-scatter.19.cloned.1.call-start = ((), (), s32[]{:S(2)}) async-start(), calls=%async_computation.17 | async-start | bytes 3932160 | tf_op jit(solution)/shard_map/reduce_scatter | solution.py:258
  290.0 434.7 %reduce-scatter.21.cloned.1.call-start = ((), (), s32[]{:S(2)}) async-start(), calls=%async_computation.18 | async-start | bytes 3932160 | tf_op jit(solution)/shard_map/reduce_scatter | solution.py:261
  292.6 373.8 %copy-start.41 = (f32[128]{0:T(128)S(1)}, f32[128]{0:T(128)}, u32[]{:S(2)}) copy-start(f32[128]{0:T(128)} %copy-done.40) | copy-start | bytes 1540
  292.6 373.8 %copy-start.45 = (f32[128]{0:T(128)S(1)}, f32[128]{0:T(128)}, u32[]{:S(2)}) copy-start(f32[128]{0:T(128)} %copy-done.44) | copy-start | bytes 1540
  292.6 374.2 %copy-start.28 = (f32[128,256]{1,0:T(8,128)S(1)}, f32[128,256]{1,0:T(8,128)}, u32[]{:S(2)}) copy-start(f32[128,256]{1,0:T(8,128)} %copy-done.27) | copy-start | bytes 393220
  292.6 374.2 %copy-start.43 = (f32[128]{0:T(128)S(1)}, f32[128]{0:T(128)}, u32[]{:S(2)}) copy-start(f32[128]{0:T(128)} %copy-done.42) | copy-start | bytes 1540
  292.7 375.8 %copy-start.5 = (bf16[640,1024]{1,0:T(8,128)(2,1)S(1)}, bf16[640,1024]{1,0:T(8,128)(2,1)}, u32[]{:S(2)}) copy-start(bf16[640,1024]{1,0:T(8,128)(2,1)} %all-gather.13.cloned.1.call-done) | copy-start | bytes 3932164
  292.7 449.3 %reduce-scatter.23.cloned.1.call-start = ((), (), s32[]{:S(2)}) async-start(), calls=%async_computation.19 | async-start | bytes 3932160 | tf_op jit(solution)/shard_map/reduce_scatter | solution.py:264
  295.1 448.1 %copy-start.23 = (bf16[640,256]{1,0:T(8,128)(2,1)S(1)}, bf16[640,256]{1,0:T(8,128)(2,1)}, u32[]{:S(2)}) copy-start(bf16[640,256]{1,0:T(8,128)(2,1)} %copy-done.22) | copy-start | bytes 983044
  295.1 460.9 %reduce-scatter.25.cloned.1.call-start = ((), (), s32[]{:S(2)}) async-start(), calls=%async_computation.21 | async-start | bytes 491520
  666.4 79.2 %copy-start.39 = (bf16[640]{0:T(1024)(128)(2,1)S(1)}, bf16[640]{0:T(1024)(128)(2,1)}, u32[]{:S(2)}) copy-start(bf16[640]{0:T(1024)(128)(2,1)} %get-tuple-element.17) | copy-start | bytes 3844
  666.5 79.2 %copy-start.47 = (bf16[256]{0:T(256)(128)(2,1)S(1)}, bf16[256]{0:T(256)(128)(2,1)}, u32[]{:S(2)}) copy-start(bf16[256]{0:T(256)(128)(2,1)} %get-tuple-element.15) | copy-start | bytes 1540
  666.5 82.0 %copy-start.11 = (f32[128,640]{1,0:T(8,128)S(1)}, f32[128,640]{1,0:T(8,128)}, u32[]{:S(2)}) copy-start(f32[128,640]{1,0:T(8,128)} %copy-done.10) | copy-start | bytes 983044
  668.4 102.2 %reduce-scatter.27.cloned.1.call-start = ((), (), s32[]{:S(2)}) async-start(), calls=%async_computation.22 | async-start | bytes 491520
  (40 other events, 730.8 us)
Sparse Core Ops, SparseCore 0:
  9.7 14.5 all-gather.12
  27.7 70.3 all-gather.22
  101.6 66.4 all-gather.10
  169.6 9.5 all-gather.14
  180.6 15.3 all-gather.16
  197.6 15.4 all-gather.18
  214.7 15.3 all-gather.20
  275.0 390.4 reduce-scatter.12
  668.4 6.0 reduce-scatter.14
  677.4 12.8 reduce-scatter.16
  693.2 14.2 reduce-scatter.18
  710.4 14.2 reduce-scatter.20
  727.6 14.2 reduce-scatter.22
  744.3 11.7 reduce-scatter.24
  758.8 11.7 reduce-scatter.26
where the time goes:
time: 1210 us; the launch traced here: 1200 us
  waiting for transfers between devices  615 us (51%)
  blocking collectives  436 us (36%)
  matrix products  83.8 us (7%)
  other arithmetic  30.5 us (3%)
  local copies, waits for them, and re-layouts  17.7 us (1%)
  between operations  17.2 us (1%)
    psum x1, blocking collectives, per_device(): lax.psum((half_query, half_key, half_value, half_out, half_gate, half_up,...  422 us
    reduce_scatter x1, waiting for transfers between devices, per_device(): kv_mine = lax.psum_scatter(kv_terms, 'ctx', scatter_dimension=0, tiled=True)  369 us
    all_gather x1, waiting for transfers between devices, per_device(): lax.all_gather(key_rot, 'ctx', axis=0, tiled=True)  55.2 us
    all_gather x1, waiting for transfers between devices, per_device(): lax.all_gather(value_bf, 'ctx', axis=0, tiled=True)  51.7 us
    dot_general x21, matrix products, dot_f32(): return jnp.dot(left, right, preferred_element_type=jnp.float32)  31.7 us
  transfers between devices with their start and end apart: 15, of which 14 were waited for; matrix products, arithmetic and copies ran while one was open for 7% of the time, Pallas kernels for 0%

commit v1 on v0

v1 whole, which is shorter than its diff:
```python
import jax
import jax.numpy as jnp
from jax import lax
from jax.sharding import Mesh
from jax.sharding import PartitionSpec as P

HEADS = 4
HDIM = 256
CTX = ("z", "x", "y")

epsilon = 1e-06
theta_base = 1000000.0
bf16 = jnp.bfloat16
f32 = jnp.float32


def rms_forward(values, gain_w):
    factor = lax.rsqrt(jnp.mean(values * values, axis=-1, keepdims=True) + epsilon)
    return (values * factor * (1.0 + gain_w), factor)


def rms_backward(values, factor, gain_w, grad_out):
    weighted = grad_out * (1.0 + gain_w)
    inner = jnp.mean(weighted * values, axis=-1, keepdims=True)
    grad_in = factor * (weighted - values * factor * factor * inner)
    grad_gain = jnp.sum((grad_out * values * factor).reshape(-1, values.shape[-1]), axis=0)
    return (grad_in, grad_gain)


def rotary_tables(positions, width):
    half_width = width // 2
    frequency = theta_base ** (-jnp.arange(half_width, dtype=f32) * 2.0 / width)
    angles = positions.astype(f32)[:, None] * frequency[None, :]
    return (jnp.cos(angles), jnp.sin(angles))


def rotate(values, cos_tab, sin_tab):
    half = values.shape[-1] // 2
    a, b = values[..., :half], values[..., half:]
    return jnp.concatenate([a * cos_tab - b * sin_tab, b * cos_tab + a * sin_tab], axis=-1)


def rotate_back(grads, cos_tab, sin_tab):
    half = grads.shape[-1] // 2
    a, b = grads[..., :half], grads[..., half:]
    return jnp.concatenate([a * cos_tab + b * sin_tab, b * cos_tab - a * sin_tab], axis=-1)


def block_positions(block_ids, half_rows):
    offsets = jnp.arange(half_rows, dtype=jnp.int32)
    return (block_ids[:, None] * half_rows + offsets[None, :]).reshape(-1)


def dot_f32(left, right):
    return jnp.dot(left, right, preferred_element_type=f32)


def dot_nt(left, right):
    return lax.dot_general(left, right, (((1,), (1,)), ((), ())), preferred_element_type=f32)


def dot_tn(left, right):
    return lax.dot_general(left, right, (((0,), (0,)), ((), ())), preferred_element_type=f32)


def swap(values):
    return lax.ppermute(values, "wsh", [(0, 1), (1, 0)])


def attention_forward(query, keys, vals, query_pos, key_pos):
    scores = dot_nt(query, keys) * HDIM ** (-0.5)
    scores = jnp.where(key_pos[None, :] <= query_pos[:, None], scores, -1e30)
    top = jnp.max(scores, axis=-1, keepdims=True)
    shifted = jnp.exp(scores - top)
    totals = jnp.sum(shifted, axis=-1, keepdims=True)
    probs = (shifted / totals).astype(bf16)
    return dot_f32(probs, vals).astype(bf16), top + jnp.log(totals)


def attention_backward(query, keys, vals, query_pos, key_pos, grads, log_total, delta):
    scores = dot_nt(query, keys) * HDIM ** (-0.5)
    scores = jnp.where(key_pos[None, :] <= query_pos[:, None], scores, -1e30)
    probs = jnp.exp(scores - log_total)
    grad_probs = dot_nt(grads, vals)
    grad_scores = (probs * (grad_probs - delta)).astype(bf16)
    grad_query = dot_f32(grad_scores, keys) * HDIM ** (-0.5)
    grad_key = dot_tn(grad_scores, query) * HDIM ** (-0.5)
    grad_value = dot_tn(probs.astype(bf16), grads)
    return grad_query, jnp.concatenate([grad_key.astype(bf16), grad_value.astype(bf16)], axis=1)


def gather_ctx(block):
    return lax.all_gather(block, CTX, axis=0, tiled=True)


def scatter_sum(parts):
    got = lax.all_to_all(parts.reshape(64, 128, -1), CTX, split_axis=0, concat_axis=0, tiled=True)
    return jnp.sum(got.astype(f32), axis=0)


def small_sum(values):
    rows = values.shape[0] // 64
    got = lax.all_to_all(values.reshape(64, rows, -1), CTX, split_axis=0, concat_axis=0, tiled=True)
    mine = jnp.sum(got.astype(f32), axis=0).astype(values.dtype)
    wide = jnp.broadcast_to(mine[None], (64,) + mine.shape)
    out = lax.all_to_all(wide, CTX, split_axis=0, concat_axis=0, tiled=True)
    return out.reshape(values.shape)


def per_device(
    block_input,
    cotangent,
    pair_blocks,
    w_query,
    w_key,
    w_value,
    w_out,
    w_gate,
    w_up,
    w_down,
    attn_pre_gain,
    query_gain,
    key_gain,
    attn_post_gain,
    ffw_pre_gain,
    ffw_post_gain,
):
    rows = block_input.shape[1]
    rank = lax.axis_index(CTX)
    first = lax.axis_index("wsh") == 0

    def ordered(own, other, axis):
        return jnp.where(
            first,
            jnp.concatenate([own, other], axis=axis),
            jnp.concatenate([other, own], axis=axis),
        )

    resid_in = block_input[0].astype(f32)
    grad_top = cotangent[0]
    query_pos = block_positions(lax.dynamic_slice_in_dim(pair_blocks, rank, 1, 0)[0], rows // 2)
    key_pos = block_positions(pair_blocks.reshape(-1), rows // 2)
    cos_tab, sin_tab = rotary_tables(query_pos, HDIM)

    gains_own = jnp.concatenate(
        [attn_pre_gain, attn_post_gain, ffw_pre_gain, ffw_post_gain, query_gain, key_gain]
    )[None]
    gains_other = swap(gains_own)
    kv_own = jnp.concatenate([w_key, w_value], axis=1)
    kv_other = swap(kv_own)

    def gain(start, width):
        return ordered(
            gains_own[0, start : start + width], gains_other[0, start : start + width], 0
        ).astype(f32)[None]

    gain_one, gain_two, gain_three, gain_four = (gain(320 * i, 320) for i in range(4))
    gain_query, gain_key = gain(1280, 128), gain(1408, 128)
    key_w = ordered(kv_own[:, :128], kv_other[:, :128], 1)
    value_w = ordered(kv_own[:, 128:], kv_other[:, 128:], 1)

    normed_one, factor_one = rms_forward(resid_in, gain_one)
    attn_in = normed_one.astype(bf16)
    key_raw = dot_f32(attn_in, key_w)
    value_bf = dot_f32(attn_in, value_w).astype(bf16)
    key_normed, key_factor = rms_forward(key_raw, gain_key)
    key_rot = rotate(key_normed, cos_tab, sin_tab).astype(bf16)
    kv_all = gather_ctx(jnp.concatenate([key_rot, value_bf], axis=1))
    key_all, value_all = kv_all[:, :HDIM], kv_all[:, HDIM:]

    query_w = (w_query, swap(w_query))
    out_w = (w_out, swap(w_out))
    gate_w = (w_gate, swap(w_gate))
    up_w = (w_up, swap(w_up))
    down_w = (w_down, swap(w_down))

    def heads_first(pair):
        return jnp.concatenate(
            [half[:, HDIM * h : HDIM * (h + 1)] for half in pair for h in range(2)], axis=0
        )

    def heads_last(stacked):
        return tuple(
            jnp.concatenate([stacked[rows * h : rows * (h + 1)] for h in (2 * p, 2 * p + 1)], axis=1)
            for p in range(2)
        )

    cos4, sin4 = jnp.tile(cos_tab, (HEADS, 1)), jnp.tile(sin_tab, (HEADS, 1))
    query_raw = heads_first(tuple(dot_f32(attn_in, half) for half in query_w))
    query_normed, query_factor = rms_forward(query_raw, gain_query)
    query_rot = rotate(query_normed, cos4, sin4).astype(bf16)
    pos4 = jnp.tile(query_pos, HEADS)
    attn_heads, log_total = attention_forward(query_rot, key_all, value_all, pos4, key_pos)
    attn_out = heads_last(attn_heads)
    attn_proj = dot_f32(attn_out[0], out_w[0]) + dot_f32(attn_out[1], out_w[1])
    normed_two, factor_two = rms_forward(attn_proj, gain_two)
    mid = resid_in + normed_two
    normed_three, factor_three = rms_forward(mid, gain_three)
    ffw_in = normed_three.astype(bf16)

    gate = [dot_f32(ffw_in, half) for half in gate_w]
    up_val = [dot_f32(ffw_in, half) for half in up_w]
    acts = [jax.vjp(lambda inner: jax.nn.gelu(inner, approximate=True), g) for g in gate]
    hidden = [(act[0] * up).astype(bf16) for act, up in zip(acts, up_val)]
    ffw_proj = dot_f32(hidden[0], down_w[0]) + dot_f32(hidden[1], down_w[1])
    normed_four, factor_four = rms_forward(ffw_proj, gain_four)
    block_output = mid + normed_four

    grad_ffw, grad_gain_four = rms_backward(ffw_proj, factor_four, gain_four, grad_top)
    grad_ffw_bf = grad_ffw.astype(bf16)
    grad_hidden = [dot_nt(grad_ffw_bf, half) for half in down_w]
    grad_gate = [
        act[1](gh * up)[0].astype(bf16) for act, gh, up in zip(acts, grad_hidden, up_val)
    ]
    grad_up = [(gh * act[0]).astype(bf16) for act, gh in zip(acts, grad_hidden)]
    grad_ffw_in = (
        dot_nt(grad_gate[0], gate_w[0])
        + dot_nt(grad_gate[1], gate_w[1])
        + dot_nt(grad_up[0], up_w[0])
        + dot_nt(grad_up[1], up_w[1])
    )
    grad_mid_part, grad_gain_three = rms_backward(mid, factor_three, gain_three, grad_ffw_in)
    grad_mid = grad_top + grad_mid_part
    grad_proj, grad_gain_two = rms_backward(attn_proj, factor_two, gain_two, grad_mid)
    grad_proj_bf = grad_proj.astype(bf16)
    grad_attn = tuple(dot_nt(grad_proj_bf, half).astype(bf16) for half in out_w)
    grad_heads = heads_first(grad_attn)

    def both(own, other):
        return jnp.concatenate([own, swap(other)], axis=0)

    ffw_in2 = both(ffw_in, ffw_in)
    grad_w_down = dot_tn(both(hidden[0], hidden[1]), both(grad_ffw_bf, grad_ffw_bf))
    grad_w_gate = dot_tn(ffw_in2, both(grad_gate[0], grad_gate[1]))
    grad_w_up = dot_tn(ffw_in2, both(grad_up[0], grad_up[1]))
    grad_w_out = dot_tn(both(attn_out[0], attn_out[1]), both(grad_proj_bf, grad_proj_bf))
    attn_in2 = both(attn_in, attn_in)

    delta = jnp.sum(grad_heads.astype(f32) * attn_heads.astype(f32), axis=-1, keepdims=True)
    grad_query, kv_terms = attention_backward(
        query_rot, key_all, value_all, pos4, key_pos, grad_heads, log_total, delta
    )
    grad_query_raw, grad_gain_query = rms_backward(
        query_raw, query_factor, gain_query, rotate_back(grad_query, cos4, sin4)
    )
    grad_query_bf = heads_last(grad_query_raw.astype(bf16))
    grad_w_query = dot_tn(attn_in2, both(grad_query_bf[0], grad_query_bf[1]))
    big = tuple(
        g.astype(bf16) for g in (grad_w_query, grad_w_out, grad_w_gate, grad_w_up, grad_w_down)
    )
    sum_query, sum_out, sum_gate, sum_up, sum_down = (
        g.astype(f32) for g in lax.psum(big, CTX)
    )

    kv_mine = scatter_sum(kv_terms)
    grad_key_raw, grad_gain_key = rms_backward(
        key_raw, key_factor, gain_key, rotate_back(kv_mine[:, :HDIM], cos_tab, sin_tab)
    )
    grad_key_bf = grad_key_raw.astype(bf16)
    grad_value_bf = kv_mine[:, HDIM:].astype(bf16)

    def mine_other(full):
        a, b = full[:, :128], full[:, 128:]
        return jnp.where(first, a, b), jnp.where(first, b, a)

    key_m, key_o = mine_other(grad_key_bf)
    val_m, val_o = mine_other(grad_value_bf)
    grad_kv2 = both(
        jnp.concatenate([key_m, val_m], axis=1), jnp.concatenate([key_o, val_o], axis=1)
    )
    grad_w_kv = dot_tn(grad_kv2, attn_in2)

    grad_attn_in = (
        dot_nt(grad_query_bf[0], query_w[0])
        + dot_nt(grad_query_bf[1], query_w[1])
        + dot_nt(grad_key_bf, key_w)
        + dot_nt(grad_value_bf, value_w)
    )
    grad_in_part, grad_gain_one = rms_backward(resid_in, factor_one, gain_one, grad_attn_in)
    input_grad = grad_mid + grad_in_part

    gain_grads = (
        grad_gain_one,
        grad_gain_two,
        grad_gain_three,
        grad_gain_four,
        grad_gain_query,
        grad_gain_key,
    )
    g_own = jnp.concatenate([jnp.where(first, g[: g.size // 2], g[g.size // 2 :]) for g in gain_grads])
    g_other = jnp.concatenate([jnp.where(first, g[g.size // 2 :], g[: g.size // 2]) for g in gain_grads])
    g_sum = g_own + swap(g_other[None])[0]
    g_block = jnp.concatenate([g_sum, jnp.zeros((1024,), f32)]).reshape(64, 40).astype(bf16)
    late = jnp.concatenate([grad_w_kv.astype(bf16).reshape(64, 2560), g_block], axis=1)
    late = small_sum(late).astype(f32)
    sum_kv = late[:, :2560].reshape(256, 640)
    sum_gains = late[:, 2560:].reshape(-1)
    return (
        block_output[None],
        input_grad[None],
        sum_query,
        sum_kv[:128].T,
        sum_kv[128:].T,
        sum_out,
        sum_gate,
        sum_up,
        sum_down,
        sum_gains[:320],
        sum_gains[1280:1408],
        sum_gains[1408:1536],
        sum_gains[320:640],
        sum_gains[640:960],
        sum_gains[960:1280],
    )


def solution(mesh):
    grid = Mesh(mesh.devices.reshape(4, 4, 4, 2), ("z", "x", "y", "wsh"))
    tokens = P("wsh", CTX, None)
    cols, rows, vec = P(None, "wsh"), P("wsh", None), P("wsh")
    return jax.shard_map(
        per_device,
        mesh=grid,
        in_specs=(tokens, tokens, P(), cols, cols, cols, rows, cols, cols, rows) + (vec,) * 6,
        out_specs=(tokens, tokens, cols, cols, cols, rows, cols, cols, rows) + (vec,) * 6,
        check_vma=False,
    )
```

time: 1210 us -> 485 us (0.40)
  blocking collectives: 436 us -> 0 us
  waiting for transfers between devices: 615 us -> 285 us
  starting transfers between devices: 0.86 us -> 31.2 us
  other arithmetic: 30.5 us -> 42.9 us
    reduce_scatter x6 -> x0, waiting for transfers between devices: 442 us -> none  [the longest x1 369 us: per_device(): kv_mine = lax.psum_scatter(kv_terms, 'ctx', scatter_dimension=0, tiled=True)]
    psum x1 -> x0, blocking collectives: 422 us -> none  [per_device(): lax.psum((half_query, half_key, half_value, half_out, half_gate, half_up,...]
    all_to_all x0 -> x3, waiting for transfers between devices: none -> 109 us  [the longest x1 97.9 us: scatter_sum(): lax.all_to_all(parts.reshape(64, 128, -1), CTX, split_axis=0, concat_axis...]
    psum x0 -> x1, waiting for transfers between devices: none -> 99.7 us  [per_device(): lax.psum(big, CTX)]
    all_gather x7 -> x1, waiting for transfers between devices: 151 us -> 75.5 us  [gather_ctx(): return lax.all_gather(block, CTX, axis=0, tiled=True)]
    all_to_all x0 -> x3, starting transfers between devices: none -> 25.9 us  [the longest x1 9.2 us: small_sum(): lax.all_to_all(values.reshape(64, rows, -1), CTX, split_axis=0, concat_ax...]
    unnamed x17 -> x2, waiting for transfers between devices: 22.4 us -> 0.03 us
    dot_general x27 -> x36, matrix products: 83.8 us -> 82.5 us  [the longest x14 35.8 us: dot_nt(): lax.dot_general(left, right, (((1,), (1,)), ((), ())), preferred_element_...]
  transfers between devices with their start and end apart: 15 -> 23, of which waited for: 14 -> 6; matrix products, arithmetic and copies ran while one was open for 7% -> 18% of each run, Pallas kernels for 0% -> 0%
where the time goes in v1:
time: 485 us; the launch traced here: 476 us
  waiting for transfers between devices  285 us (59%)
  matrix products  82.5 us (17%)
  other arithmetic  42.9 us (9%)
  starting transfers between devices  31.2 us (6%)
  local copies, waits for them, and re-layouts  19.3 us (4%)
  between operations  15.8 us (3%)
    psum x1, waiting for transfers between devices, per_device(): lax.psum(big, CTX)  99.7 us
    all_to_all x1, waiting for transfers between devices, scatter_sum(): lax.all_to_all(parts.reshape(64, 128, -1), CTX, split_axis=0, concat_axis...  97.9 us
    all_gather x1, waiting for transfers between devices, gather_ctx(): return lax.all_gather(block, CTX, axis=0, tiled=True)  75.5 us
    dot_general x14, matrix products, dot_nt(): lax.dot_general(left, right, (((1,), (1,)), ((), ())), preferred_element_...  35.8 us
    dot_general x14, matrix products, dot_f32(): return jnp.dot(left, right, preferred_element_type=f32)  31.5 us
    dot_general x8, matrix products, dot_tn(): lax.dot_general(left, right, (((0,), (0,)), ((), ())), preferred_element_...  15.1 us
    all_to_all x1, waiting for transfers between devices, small_sum(): out = lax.all_to_all(wide, CTX, split_axis=0, concat_axis=0, tiled=True)  10.7 us
    convert_element_type x5, other arithmetic, per_device(): g.astype(f32)  9.98 us
  transfers between devices with their start and end apart: 23, of which 6 were waited for; matrix products, arithmetic and copies ran while one was open for 18% of the time, Pallas kernels for 0%

profile of v1, /device:TPU:0, one launch (start us, length us, event | category | flops | bytes accessed | tf_op | source)
XLA Modules:
  0.0 476.2 jit_solution(2237025595340672218)
XLA Ops:
  7.2 4.3 concatenate.211
  26.4 75.5 %all-gather.2.cloned.1.call-done = bf16[8192,512]{1,0:T(8,128)(2,1)} async-done(((bf16[128,512]{1,0:T(8,128)(2,1)}), bf16[8192,512]{1,0:T(8,128)(2,1)}) %all-gather.2.cloned.1.call-update) | async-done | bytes 8388624 | tf_op jit(solution)/shard_map/all_gather | solution.py:93
  101.9 10.8 %fusion.133 = (f32[512]{0:T(512)S(1)}, f32[512,8192]{1,0:T(8,128)}) fusion(bf16[8192,512]{1,0:T(8,128)(2,1)} %all-gather.2.cloned.1.call-done, bf16[512,128]{1,0:T(8,128)(2,1)} %get-tuple-element.99, bf16[512,128]{1,0:T(8,128)(2,1)S(1)} %get-tuple-element.98, s32[512]{0:T(512)S(1)} %broadcast_bitcast_fusion, s32[8192]{0:T(1024)S(1)} %add.247), kind=kOutput, calls=%fused_computation.278 | convolution fusion | flops 2164784640 | bytes 21270528 | tf_op jit(solution)/shard_map/dot_general | solution.py:59
  112.8 8.1 %fusion = f32[512]{0:T(512)S(1)} fusion(f32[512,8192]{1,0:T(8,128)} %get-tuple-element.159, f32[512]{0:T(512)S(1)} %get-tuple-element.158), kind=kLoop, calls=%fused_computation.6 | loop fusion | flops 8388096 | bytes 16781312 | tf_op jit(solution)/shard_map/reduce_sum | solution.py:75
  120.9 9.7 %fusion.14 = bf16[512,256]{0,1:T(8,128)(2,1)S(1)} fusion(bf16[8192,512]{1,0:T(8,128)(2,1)} %all-gather.2.cloned.1.call-done, f32[512,8192]{1,0:T(8,128)} %get-tuple-element.159, f32[512]{0:T(512)S(1)} %fusion, f32[512]{0:T(512)S(1)} %get-tuple-element.158), kind=kOutput, calls=%fused_computation.27 | convolution fusion | flops 2160197632 | bytes 21237760 | tf_op jit(solution)/shard_map/dot_general | solution.py:55
  139.0 1.9 multiply_reduce_fusion.9
  143.3 2.0 fusion.139
  145.4 2.2 multiply_convert_fusion.2
  147.6 2.1 convolution_add_fusion.5
  155.8 5.2 %convolution_convert_fusion = bf16[8192,256]{0,1:T(8,128)(2,1)} fusion(f32[512,8192]{1,0:T(8,128)S(1)} %bitcast.112, f32[512]{0:T(512)S(1)} %log_add_fusion, bf16[128,256]{0,1:T(8,128)(2,1)S(1)} %get-tuple-element.131, bf16[128,256]{0,1:T(8,128)(2,1)S(1)} %get-tuple-element.130, bf16[128,256]{0,1:T(8,128)(2,1)} %copy-done.20, bf16[128,256]{0,1:T(8,128)(2,1)} %copy-done.19), kind=kOutput, calls=%fused_computation.8 | convolution fusion | flops 2159017984 | bytes 21235712 | tf_op jit(solution)/shard_map/dot_general | solution.py:63
  161.0 10.3 %multiply_convert_fusion = bf16[512,8192]{1,0:T(8,128)(2,1)S(1)} fusion(f32[512,8192]{1,0:T(8,128)} %get-tuple-element.159, f32[512]{0:T(512)S(1)} %multiply_reduce_fusion.2, f32[512]{0:T(512)S(1)} %log_add_fusion, bf16[8192,512]{1,0:T(8,128)(2,1)} %all-gather.2.cloned.1.call-done, bf16[128,256]{0,1:T(8,128)(2,1)S(1)} %get-tuple-element.131, ...), kind=kOutput, calls=%fused_computation.1 | convolution fusion | flops 2165309440 | bytes 29626368 | tf_op jit(solution)/shard_map/dot_general | solution.py:59
  171.3 2.4 fusion.2
  176.5 4.4 copy_bitcast_fusion
  180.9 9.0 %all-to-all-start = ((bf16[64,128,512]{1,2,0:T(8,128)(2,1)}), bf16[64,128,512]{1,2,0:T(8,128)(2,1)}, u32[]{:S(2)}, u32[]{:S(2)}) async-start(bf16[64,128,512]{1,2,0:T(8,128)(2,1)} %copy_bitcast_fusion), calls=%async_computation | async-start | bytes 16777216 | tf_op jit(solution)/shard_map/all_to_all | solution.py:97
  190.1 6.9 %fusion.11 = f32[512,256]{1,0:T(8,128)S(1)} fusion(bf16[512,8192]{1,0:T(8,128)(2,1)} %copy-done.1, bf16[8192,512]{1,0:T(8,128)(2,1)} %all-gather.2.cloned.1.call-done), kind=kOutput, calls=%fused_computation.26 | convolution fusion | flops 2147614720 | bytes 13107200 | tf_op jit(solution)/shard_map/dot_general | solution.py:55
  210.9 97.9 %all-to-all-done = bf16[64,128,512]{1,2,0:T(8,128)(2,1)} async-done(((bf16[64,128,512]{1,2,0:T(8,128)(2,1)}), bf16[64,128,512]{1,2,0:T(8,128)(2,1)}, u32[]{:S(2)}, u32[]{:S(2)}) %all-to-all-start) | async-done | bytes 8388640 | tf_op jit(solution)/shard_map/all_to_all | solution.py:97
  308.8 4.7 convert_reduce_fusion
  319.8 9.2 %all-to-all-start.1 = ((bf16[64,2,1300]{2,1,0:T(2,128)(2,1)}), bf16[64,2,1300]{2,1,0:T(2,128)(2,1)S(1)}, u32[]{:S(2)}, u32[]{:S(2)}) async-start(bf16[64,2,1300]{2,1,0:T(2,128)(2,1)} %reshape.477), calls=%async_computation.1 | async-start | bytes 720896 | tf_op jit(solution)/shard_map/all_to_all | solution.py:103
  329.0 99.7 %all-reduce.4.cloned.1.call-done = (bf16[640,512]{1,0:T(8,128)(2,1)}, bf16[512,640]{1,0:T(8,128)(2,1)}, bf16[640,1024]{1,0:T(8,128)(2,1)}, bf16[640,1024]{1,0:T(8,128)(2,1)}, bf16[1024,640]{1,0:T(8,128)(2,1)}) async-done(((bf16[640,512]{1,0:T(8,128)(2,1)}, bf16[512,640]{1,0:T(8,128)(2,1)}, bf16[640,1024]{1,0:T(8,128)(2,1)}, bf16[640,1024]{1,0:T(8,128)(2,1)}, bf16[1024,640]{1,0:T(8,128)(2,1)}), ...) | async-done | bytes 5242896 | tf_op jit(solution)/shard_map/psum | solution.py:252
  428.7 2.5 convert_element_type.209
  431.2 2.2 convert_element_type.215
  440.2 2.8 reduce.22
  444.1 7.7 %all-to-all-start.2 = ((bf16[64,2,1300]{2,1,0:T(2,128)(2,1)}), bf16[64,2,1300]{2,1,0:T(2,128)(2,1)S(1)}, u32[]{:S(2)}, u32[]{:S(2)}) async-start(bf16[64,2,1300]{2,1,0:T(2,128)(2,1)} %reshape.479), calls=%async_computation.2 | async-start | bytes 720896 | tf_op jit(solution)/shard_map/all_to_all | solution.py:106
  452.7 10.7 %all-to-all-done.2 = bf16[64,2,1300]{2,1,0:T(2,128)(2,1)S(1)} async-done(((bf16[64,2,1300]{2,1,0:T(2,128)(2,1)}), bf16[64,2,1300]{2,1,0:T(2,128)(2,1)S(1)}, u32[]{:S(2)}, u32[]{:S(2)}) %all-to-all-start.2) | async-done | bytes 332832 | tf_op jit(solution)/shard_map/all_to_all | solution.py:106
  (331 shorter events, 68.2 us)
Async XLA Ops:
  7.2 94.7 %all-gather.2.cloned.1.call-start = ((), (), s32[]{:S(2)}) async-start(), calls=%async_computation.3 | async-start | bytes 8519680 | tf_op jit(solution)/shard_map/all_gather | solution.py:93
  11.5 3.9 collective-permute-start
  12.7 4.0 collective-permute-start.2
  20.6 3.4 collective-permute-start.1
  20.7 111.6 %collective-permute-start.3 = (bf16[512,640]{1,0:T(8,128)(2,1)}, bf16[512,640]{1,0:T(8,128)(2,1)}, u32[]{:S(2)}, u32[]{:S(2)}) collective-permute-start(bf16[512,640]{1,0:T(8,128)(2,1)} %param.22), channel_id=1, source_target_pairs={{0,1},{1,0},{2,3},{3,2},{4,5},{5,4},{6,7},{7,6},{8,9},{9,8},{10,11... | collective-permute-start | bytes 1966088 | tf_op jit(solution)/shard_map/ppermute | solution.py:67
  21.2 115.5 %collective-permute-start.4 = (bf16[640,1024]{1,0:T(8,128)(2,1)}, bf16[640,1024]{1,0:T(8,128)(2,1)}, u32[]{:S(2)}, u32[]{:S(2)}) collective-permute-start(bf16[640,1024]{1,0:T(8,128)(2,1)} %param.23), channel_id=1, source_target_pairs={{0,1},{1,0},{2,3},{3,2},{4,5},{5,4},{6,7},{7,6},{8,9},{9,8},{10,11... | collective-permute-start | bytes 3932168 | tf_op jit(solution)/shard_map/ppermute | solution.py:67
  21.4 117.2 %collective-permute-start.5 = (bf16[640,1024]{1,0:T(8,128)(2,1)S(1)}, bf16[640,1024]{1,0:T(8,128)(2,1)S(1)}, u32[]{:S(2)}, u32[]{:S(2)}) collective-permute-start(bf16[640,1024]{1,0:T(8,128)(2,1)S(1)} %copy-done.2), channel_id=1, source_target_pairs={{0,1},{1,0},{2,3},{3,2},{4,5},{5,4},{6,7},{7,6},{8,9},{9,8},{10,11... | collective-permute-start | bytes 3932168 | tf_op jit(solution)/shard_map/ppermute | solution.py:67
  21.8 117.2 %collective-permute-start.6 = (bf16[1024,640]{1,0:T(8,128)(2,1)}, bf16[1024,640]{1,0:T(8,128)(2,1)}, u32[]{:S(2)}, u32[]{:S(2)}) collective-permute-start(bf16[1024,640]{1,0:T(8,128)(2,1)} %param.25), channel_id=1, source_target_pairs={{0,1},{1,0},{2,3},{3,2},{4,5},{5,4},{6,7},{7,6},{8,9},{9,8},{10,11... | collective-permute-start | bytes 3932168 | tf_op jit(solution)/shard_map/ppermute | solution.py:67
  180.9 127.9 %all-to-all-start = ((bf16[64,128,512]{1,2,0:T(8,128)(2,1)}), bf16[64,128,512]{1,2,0:T(8,128)(2,1)}, u32[]{:S(2)}, u32[]{:S(2)}) async-start(bf16[64,128,512]{1,2,0:T(8,128)(2,1)} %copy_bitcast_fusion), calls=%async_computation | async-start | bytes 16777216 | tf_op jit(solution)/shard_map/all_to_all | solution.py:97
  190.0 238.7 %all-reduce.4.cloned.1.call-start = ((), (), s32[]{:S(2)}) async-start(), calls=%async_computation.4 | async-start | bytes 10485760 | tf_op jit(solution)/shard_map/psum | solution.py:252
  190.0 9.1 %collective-permute-start.7 = (bf16[128,640]{1,0:T(8,128)(2,1)S(1)}, bf16[128,640]{1,0:T(8,128)(2,1)S(1)}, u32[]{:S(2)}, u32[]{:S(2)}) collective-permute-start(bf16[128,640]{1,0:T(8,128)(2,1)S(1)} %copy-done.10), channel_id=1, source_target_pairs={{0,1},{1,0},{2,3},{3,2},{4,5},{5,4},{6,7},{7,6},{8,9},{9,8},{10,11... | collective-permute-start | bytes 491528 | tf_op jit(solution)/shard_map/ppermute | solution.py:67
  197.9 1.7 collective-permute-start.8
  198.4 2.9 collective-permute-start.12
  198.6 4.3 collective-permute-start.14
  199.0 2.0 collective-permute-start.11
  199.2 3.7 collective-permute-start.13
  199.6 4.9 %collective-permute-start.15 = (bf16[128,1024]{1,0:T(8,128)(2,1)S(1)}, bf16[128,1024]{1,0:T(8,128)(2,1)S(1)}, u32[]{:S(2)}, u32[]{:S(2)}) collective-permute-start(bf16[128,1024]{1,0:T(8,128)(2,1)S(1)} %copy-done.38), channel_id=1, source_target_pairs={{0,1},{1,0},{2,3},{3,2},{4,5},{5,4},{6,7},{7,6},{8,9},{9,8},{10,11... | collective-permute-start | bytes 786440 | tf_op jit(solution)/shard_map/ppermute | solution.py:67
  201.0 5.1 %collective-permute-start.16 = (bf16[128,1024]{1,0:T(8,128)(2,1)S(1)}, bf16[128,1024]{1,0:T(8,128)(2,1)S(1)}, u32[]{:S(2)}, u32[]{:S(2)}) collective-permute-start(bf16[128,1024]{1,0:T(8,128)(2,1)S(1)} %copy-done.24), channel_id=1, source_target_pairs={{0,1},{1,0},{2,3},{3,2},{4,5},{5,4},{6,7},{7,6},{8,9},{9,8},{10,11... | collective-permute-start | bytes 786440 | tf_op jit(solution)/shard_map/ppermute | solution.py:67
  201.3 4.8 %collective-permute-start.17 = (bf16[128,640]{1,0:T(8,128)(2,1)S(1)}, bf16[128,640]{1,0:T(8,128)(2,1)S(1)}, u32[]{:S(2)}, u32[]{:S(2)}) collective-permute-start(bf16[128,640]{1,0:T(8,128)(2,1)S(1)} %copy-done.54), channel_id=1, source_target_pairs={{0,1},{1,0},{2,3},{3,2},{4,5},{5,4},{6,7},{7,6},{8,9},{9,8},{10,11... | collective-permute-start | bytes 491528 | tf_op jit(solution)/shard_map/ppermute | solution.py:67
  210.9 103.8 %copy-start.48 = (bf16[640,128]{1,0:T(8,128)(2,1)S(1)}, bf16[640,128]{1,0:T(8,128)(2,1)}, u32[]{:S(2)}) copy-start(bf16[640,128]{1,0:T(8,128)(2,1)} %param.21) | copy-start | bytes 491524
  315.2 1.2 collective-permute-start.10
  315.4 1.5 collective-permute-start.9
  319.8 118.9 %all-to-all-start.1 = ((bf16[64,2,1300]{2,1,0:T(2,128)(2,1)}), bf16[64,2,1300]{2,1,0:T(2,128)(2,1)S(1)}, u32[]{:S(2)}, u32[]{:S(2)}) async-start(bf16[64,2,1300]{2,1,0:T(2,128)(2,1)} %reshape.477), calls=%async_computation.1 | async-start | bytes 720896 | tf_op jit(solution)/shard_map/all_to_all | solution.py:103
  444.1 19.3 %all-to-all-start.2 = ((bf16[64,2,1300]{2,1,0:T(2,128)(2,1)}), bf16[64,2,1300]{2,1,0:T(2,128)(2,1)S(1)}, u32[]{:S(2)}, u32[]{:S(2)}) async-start(bf16[64,2,1300]{2,1,0:T(2,128)(2,1)} %reshape.479), calls=%async_computation.2 | async-start | bytes 720896 | tf_op jit(solution)/shard_map/all_to_all | solution.py:106
  (75 other events, 1544.2 us)
Sparse Core Ops, SparseCore 0:
  20.7 81.1 all-gather.1
  207.9 220.7 all-reduce.3
